TPU v7x, 128 devices: a whole 4x4x4 slice. The times are simulated.
128 devices in a mesh: row: 8 (over z, core), col: 8 (over x, y_hi), depth: 2 (over y_lo).
Axes of the slice: x: 4, y: 4 (y_hi: 2, y_lo: 2; y = y_hi * 2 + y_lo), z: 4, core: 2. Of those that a mesh axis runs over, the one named last changes fastest.
Arguments:
- amplitudes: bfloat16 [616, 616, 1024], P('col', 'row', 'depth'), may hold values from -6 to 6
- ladder_ints: bfloat16 [616, 616, 1024], P('col', 'row', 'depth'), may hold values from -0.013671875 to 0.013671875
- cycle_ints: bfloat16 [616, 32, 2048], P('row', None, 'col'), may hold values from -0.0625 to 0.0625
- ladder_source: float32 [1024, 1024], P(('row', 'col'), 'depth'), may hold values from -6 to 6
- cycle_source: float32 [616, 32, 2048], P('col', 'depth', 'row'), may hold values from -6 to 6
- occ_energy: float32 [32], replicated, may hold values from -2 to -0.4
- virt_energy: float32 [616], replicated, may hold values from 0.2 to 3
- pair_energy: float32 [1024], P(('row', 'col')), may hold values from 0.4 to 6
- slice_energy: float32 [64], replicated, may hold values from 0.2 to 3
Outputs:
- ladder_new: float32 [1024, 1024], P(('row', 'col'), 'depth')
- cycle_new: float32 [616, 32, 2048], P('col', 'depth', 'row')
All inputs are finite; a program needn't handle non-finite values.
Results may differ from a plain program's by a relative error of at most 0.0003.
Values may be sent and summed in bfloat16 or wider, within the bound.
No kernel may reach another device: no remote copies, remote signals or barrier semaphores. Data moves between devices by JAX's collectives and lax.ppermute only.
A program may use at most 128 MiB of HBM per device.

v0:
```python
import jax
import jax.numpy as jnp
from jax import lax
from jax.sharding import PartitionSpec as P


def body(
    amplitudes,
    ladder_ints,
    cycle_ints,
    ladder_source,
    cycle_source,
    occ_energy,
    virt_energy,
    pair_energy,
    slice_energy,
):
    virt_col, virt_row, pair_occ = amplitudes.shape
    occ_all = occ_energy.shape[0]
    occ_dev = pair_occ // occ_all
    inner = virt_col * virt_row
    flat_amp = amplitudes.reshape(inner, pair_occ)
    piece = lax.all_gather(ladder_ints, "depth", axis=2, tiled=True)
    partial_sum = lax.dot_general(
        piece.reshape(inner, piece.shape[2]),
        flat_amp,
        (((0,), (0,)), ((), ())),
        preferred_element_type=jnp.float32,
    )
    ladder_sum = lax.psum_scatter(partial_sum, ("row", "col"), scatter_dimension=0, tiled=True)
    occ_mine = lax.dynamic_slice_in_dim(occ_energy, lax.axis_index("depth") * occ_dev, occ_dev)
    occ_pairs = (occ_mine[:, None] + occ_energy[None, :]).reshape(pair_occ)
    ladder_den = occ_pairs[None, :] - pair_energy[:, None]
    ladder_new = (ladder_source + ladder_sum) / ladder_den
    slice_size = slice_energy.shape[0]
    cycle_amp = (
        amplitudes.reshape(virt_col, virt_row, occ_dev, occ_all)
        .transpose(0, 2, 1, 3)
        .reshape(virt_col * occ_dev, virt_row * occ_all)
    )
    piece = lax.all_gather(cycle_ints, "col", axis=2, tiled=True)
    cycle_part = jnp.dot(
        cycle_amp,
        piece.reshape(virt_row * occ_all, piece.shape[2]),
        preferred_element_type=jnp.float32,
    )
    cycle_part = cycle_part.reshape(virt_col, occ_dev, occ_all * slice_size)
    cycle_sum = lax.psum_scatter(cycle_part, "row", scatter_dimension=2, tiled=True)
    occ_share = cycle_sum.shape[2] // slice_size
    occ_rows = lax.dynamic_slice_in_dim(occ_energy, lax.axis_index("row") * occ_share, occ_share)
    virt_mine = lax.dynamic_slice_in_dim(virt_energy, lax.axis_index("col") * virt_col, virt_col)
    jb_part = (occ_rows[:, None] - slice_energy[None, :]).reshape(occ_share * slice_size)
    cycle_den = occ_mine[None, :, None] - virt_mine[:, None, None] + jb_part[None, None, :]
    cycle_new = (cycle_source + cycle_sum) / cycle_den
    return (ladder_new, cycle_new)


def solution(mesh):
    placed = (
        P("col", "row", "depth"),
        P("col", "row", "depth"),
        P("row", None, "col"),
        P(("row", "col"), "depth"),
        P("col", "depth", "row"),
        P(),
        P(),
        P(("row", "col")),
        P(),
    )
    return jax.shard_map(
        body,
        mesh=mesh,
        in_specs=placed,
        out_specs=(P(("row", "col"), "depth"), P("col", "depth", "row")),
        check_vma=False,
    )
```

profile of v0, /device:TPU:1, one launch (start us, length us, event | category | flops | bytes accessed | tf_op | source)
XLA Modules:
  0.0 716.0 jit_solution(5468249073596840638)
XLA Ops:
  7.2 0.0 copy-start
  7.2 0.0 all-gather.3.cloned.1.call-start
  7.2 0.7 all-gather.3.cloned.1.call-update
  7.9 0.0 all-gather.5.cloned.1.call-start
  8.0 0.5 copy-done
  8.5 1.8 copy.14
  10.2 0.0 all-gather.5.cloned.1.call-update
  10.2 0.0 reduce-scatter.3.cloned.1.call-start
  10.3 11.4 %copy.13 = bf16[77,77,512]{1,2,0:T(8,128)(2,1)} copy(bf16[77,77,512]{2,1,0:T(8,128)(2,1)} %param.9) | data formatting | bytes 12142592 | tf_op args[0]
  21.7 146.7 %all-gather.3.cloned.1.call-done = bf16[77,77,1024]{2,1,0:T(8,128)(2,1)} async-done(((bf16[77,77,512]{2,1,0:T(8,128)(2,1)}), bf16[77,77,1024]{2,1,0:T(8,128)(2,1)}) %all-gather.3.cloned.1.call-update) | async-done | bytes 12142608 | tf_op jit(solution)/shard_map/all_gather | solution.py:23
  168.3 12.8 %convolution_bitcast_fusion = f32[1024,512]{1,0:T(8,128)} fusion(bf16[77,77,1024]{2,1,0:T(8,128)(2,1)} %all-gather.3.cloned.1.call-done, bf16[77,77,512]{2,1,0:T(8,128)(2,1)} %param.9), kind=kOutput, calls=%fused_computation.4 | convolution fusion | flops 6217007104 | bytes 20311040 | tf_op jit(solution)/shard_map/dot_general | solution.py:24
  181.1 0.0 reduce-scatter.3.cloned.1.call-update
  181.1 0.0 reduce-scatter.5.cloned.1.call-start
  181.2 131.4 %all-gather.5.cloned.1.call-done = bf16[77,32,2048]{2,0,1:T(8,128)(2,1)} async-done(((bf16[77,32,256]{2,0,1:T(8,128)(2,1)}), bf16[77,32,2048]{2,0,1:T(8,128)(2,1)}) %all-gather.5.cloned.1.call-update) | async-done | bytes 10092560 | tf_op jit(solution)/shard_map/all_gather | solution.py:41
  312.5 34.6 %fusion.3 = f32[77,16,2048]{2,1,0:T(8,128)} fusion(bf16[77,32,2048]{2,0,1:T(8,128)(2,1)} %all-gather.5.cloned.1.call-done, bf16[77,16,77,32]{2,3,1,0:T(8,128)(2,1)} %bitcast.15), kind=kOutput, calls=%fused_computation.3 | convolution fusion | flops 12434014208 | bytes 26256384 | tf_op jit(solution)/shard_map/dot_general | solution.py:42
  347.2 0.0 copy-start.3
  347.2 0.0 copy-start.1
  347.2 0.0 reduce-scatter.5.cloned.1.call-update
  347.2 0.6 copy-done.4
  347.8 0.1 dynamic_slice.9
  347.9 0.1 broadcast_add_fusion
  348.0 0.1 add.57
  348.0 0.1 dynamic_slice.11
  348.1 0.0 copy-done.5
  348.1 0.1 broadcast_subtract_fusion.1
  348.2 0.1 sub.60
  348.3 0.8 dynamic_slice.10
  349.0 0.1 broadcast_subtract_fusion
  349.1 290.9 %reduce-scatter.3.cloned.1.call-done = f32[16,512]{1,0:T(8,128)} async-done(((f32[1024,512]{1,0:T(8,128)}), f32[16,512]{1,0:T(8,128)}) %reduce-scatter.3.cloned.1.call-update) | async-done | bytes 32784 | tf_op jit(solution)/shard_map/reduce_scatter | solution.py:30
  640.0 1.5 subtract_divide_fusion
  641.5 65.4 %reduce-scatter.5.cloned.1.call-done = f32[77,16,256]{2,1,0:T(8,128)} async-done(((f32[77,16,2048]{2,1,0:T(8,128)}), f32[77,16,256]{2,1,0:T(8,128)}) %reduce-scatter.5.cloned.1.call-update) | async-done | bytes 1261584 | tf_op jit(solution)/shard_map/reduce_scatter | solution.py:48
  706.9 2.6 add_divide_fusion
  (6 shorter events, 0.0 us)
Async XLA Ops:
  7.2 1.3 copy-start
  7.2 161.2 %all-gather.3.cloned.1.call-start = ((), (), s32[]{:S(2)}) async-start(), calls=%async_computation.2 | async-start | bytes 18923520 | tf_op jit(solution)/shard_map/all_gather | solution.py:23
  7.9 304.6 %all-gather.5.cloned.1.call-start = ((), (), s32[]{:S(2)}) async-start(), calls=%async_computation.4 | async-start | bytes 11796480 | tf_op jit(solution)/shard_map/all_gather | solution.py:41
  10.2 629.8 %reduce-scatter.3.cloned.1.call-start = ((), (), s32[]{:S(2)}) async-start(), calls=%async_computation.3 | async-start | bytes 2129920 | tf_op jit(solution)/shard_map/reduce_scatter | solution.py:30
  181.1 525.8 %reduce-scatter.5.cloned.1.call-start = ((), (), s32[]{:S(2)}) async-start(), calls=%async_computation.5 | async-start | bytes 11354112 | tf_op jit(solution)/shard_map/reduce_scatter | solution.py:48
  347.2 0.7 copy-start.4
  347.2 1.0 copy-start.5
  347.2 292.8 %copy-start.2 = (f32[16,512]{1,0:T(8,128)S(1)}, f32[16,512]{1,0:T(8,128)}, u32[]{:S(2)}) copy-start(f32[16,512]{1,0:T(8,128)} %param.12) | copy-start | bytes 98308
  347.2 292.8 %copy-start.3 = (f32[16]{0:T(128)S(1)}, f32[16]{0:T(128)}, u32[]{:S(2)}) copy-start(f32[16]{0:T(128)} %param.16) | copy-start | bytes 196
  347.2 359.7 %copy-start.1 = (f32[77,16,256]{2,1,0:T(8,128)S(1)}, f32[77,16,256]{2,1,0:T(8,128)}, u32[]{:S(2)}) copy-start(f32[77,16,256]{2,1,0:T(8,128)} %param.13) | copy-start | bytes 3784708
Sparse Core Ops, SparseCore 0:
  9.7 158.6 all-gather.2
  170.5 141.9 all-gather.4
  314.9 325.0 reduce-scatter.2
  642.4 64.4 reduce-scatter.4
where the time goes:
time: 717 us; the launch traced here: 716 us
  waiting for transfers between devices  635 us (89%)
  matrix products  47.4 us (7%)
  local copies, waits for them, and re-layouts  15.3 us (2%)
  between operations  13.8 us (2%)
    reduce_scatter x1, waiting for transfers between devices, body(): lax.psum_scatter(partial_sum, ('row', 'col'), scatter_dimension=0, tiled=...  291 us
    all_gather x1, waiting for transfers between devices, body(): piece = lax.all_gather(ladder_ints, 'depth', axis=2, tiled=True)  147 us
    all_gather x1, waiting for transfers between devices, body(): piece = lax.all_gather(cycle_ints, 'col', axis=2, tiled=True)  131 us
    reduce_scatter x1, waiting for transfers between devices, body(): lax.psum_scatter(cycle_part, 'row', scatter_dimension=2, tiled=True)  65.4 us
    dot_general x1, matrix products, body(): jnp.dot(cycle_amp, piece.reshape(virt_row * occ_all, piece.shape[2]), pre...  34.6 us
  transfers between devices with their start and end apart: 4, of which 4 were waited for; matrix products, arithmetic and copies ran while one was open for 9% of the time, Pallas kernels for 0%

commit v1 on v0

--- a/solution.py
+++ b/solution.py
@@ -1,7 +1,20 @@
+import functools
 import jax
 import jax.numpy as jnp
 from jax import lax
 from jax.sharding import PartitionSpec as P
+
+
+def serve_vectors(mat, named_axis, on_dim):
+    return jnp.concatenate(
+        lax.all_to_all(
+            jnp.stack([mat] * lax.axis_size(named_axis)), named_axis, concat_axis=0, split_axis=0
+        ),
+        axis=on_dim,
+    )
+
+
+serve_roots = functools.partial(serve_vectors, named_axis="depth", on_dim=2)
 
 
 def body(
@@ -20,7 +33,7 @@
     occ_dev = pair_occ // occ_all
     inner = virt_col * virt_row
     flat_amp = amplitudes.reshape(inner, pair_occ)
-    piece = lax.all_gather(ladder_ints, "depth", axis=2, tiled=True)
+    piece = serve_roots(ladder_ints)
     partial_sum = lax.dot_general(
         piece.reshape(inner, piece.shape[2]),
         flat_amp,

time: 717 us -> 678 us (0.946)
  waiting for transfers between devices: 635 us -> 537 us
  local copies, waits for them, and re-layouts: 15.3 us -> 57.1 us
  other arithmetic: 4.25 us -> 15.5 us
  starting transfers between devices: 0.16 us -> 9.3 us
    all_to_all x0 -> x1, waiting for transfers between devices: none -> 182 us  [serve_vectors(): lax.all_to_all(jnp.stack([mat] * lax.axis_size(named_axis)), named_axis,...]
    all_gather x1 -> x0, waiting for transfers between devices: 147 us -> none  [body(): piece = lax.all_gather(ladder_ints, 'depth', axis=2, tiled=True)]
    all_gather x1, waiting for transfers between devices: 131 us -> 0.02 us  [body(): piece = lax.all_gather(cycle_ints, 'col', axis=2, tiled=True)]
    reshape x0 -> x2, local copies, waits for them, and re-layouts: none -> 27.1 us  [the longest x1 18.1 us: serve_vectors(): jnp.concatenate(lax.all_to_all(jnp.stack([mat] * lax.axis_size(named_axis...]
    unnamed x14 -> x18, local copies, waits for them, and re-layouts: 14.2 us -> 28.9 us
    another operation x0 -> x1, other arithmetic: none -> 11.2 us  [serve_vectors(): jnp.stack([mat] * lax.axis_size(named_axis))]
    all_to_all x0 -> x1, starting transfers between devices: none -> 9 us  [serve_vectors(): lax.all_to_all(jnp.stack([mat] * lax.axis_size(named_axis)), named_axis,...]
  transfers between devices with their start and end apart: 4 -> 4, of which waited for: 4 -> 3; matrix products, arithmetic and copies ran while one was open for 9% -> 16% of each run, Pallas kernels for 0% -> 0%
where the time goes in v1:
time: 678 us; the launch traced here: 677 us
  waiting for transfers between devices  537 us (79%)
  local copies, waits for them, and re-layouts  57.1 us (8%)
  matrix products  42.6 us (6%)
  between operations  15.6 us (2%)
  other arithmetic  15.5 us (2%)
  starting transfers between devices  9.3 us (1%)
    reduce_scatter x1, waiting for transfers between devices, body(): lax.psum_scatter(partial_sum, ('row', 'col'), scatter_dimension=0, tiled=...  289 us
    all_to_all x1, waiting for transfers between devices, serve_vectors(): lax.all_to_all(jnp.stack([mat] * lax.axis_size(named_axis)), named_axis,...  182 us
    reduce_scatter x1, waiting for transfers between devices, body(): lax.psum_scatter(cycle_part, 'row', scatter_dimension=2, tiled=True)  65.8 us
    dot_general x1, matrix products, body(): jnp.dot(cycle_amp, piece.reshape(virt_row * occ_all, piece.shape[2]), pre...  34.7 us
    unnamed x18, local copies, waits for them, and re-layouts  28.9 us
    reshape x1, local copies, waits for them, and re-layouts, serve_vectors(): jnp.concatenate(lax.all_to_all(jnp.stack([mat] * lax.axis_size(named_axis...  18.1 us
  transfers between devices with their start and end apart: 4, of which 3 were waited for; matrix products, arithmetic and copies ran while one was open for 16% of the time, Pallas kernels for 0%

profile of v1, /device:TPU:1, one launch (start us, length us, event | category | flops | bytes accessed | tf_op | source)
XLA Modules:
  0.0 676.9 jit_solution(7761072643385959673)
XLA Ops:
  8.0 0.0 all-gather.2.cloned.1.call-start
  8.0 3.1 copy.15
  11.1 0.0 all-gather.2.cloned.1.call-update
  11.1 11.2 %pad_maximum_fusion = bf16[2,77,77,512]{3,2,1,0:T(8,128)(2,1)} fusion(bf16[1,77,77,512]{3,2,1,0:T(8,128)(2,1)} %bitcast.23), kind=kLoop, calls=%fused_computation | loop fusion | flops 6071296 | bytes 18213888 | tf_op jit(solution)/shard_map/stack | solution.py:11
  22.3 9.0 %all-to-all-start = ((bf16[2,77,77,512]{3,2,1,0:T(8,128)(2,1)}), bf16[2,77,77,512]{3,2,1,0:T(8,128)(2,1)}, u32[]{:S(2)}, u32[]{:S(2)}) async-start(bf16[2,77,77,512]{3,2,1,0:T(8,128)(2,1)} %pad_maximum_fusion), calls=%async_computation | async-start | bytes 25231360 | tf_op jit(solution)/shard_map/all_to_all | solution.py:10
  31.3 0.0 reduce-scatter.3.cloned.1.call-start
  31.4 9.1 %reshape.84 = bf16[5929,512]{1,0:T(8,128)(2,1)} reshape(bf16[77,77,512]{2,1,0:T(8,128)(2,1)} %param.9) | data formatting | bytes 12142592 | tf_op jit(solution)/shard_map/reshape | solution.py:35
  40.5 11.4 %copy.14 = bf16[77,77,512]{1,2,0:T(8,128)(2,1)} copy(bf16[77,77,512]{2,1,0:T(8,128)(2,1)} %param.9) | data formatting | bytes 12142592 | tf_op args[0]
  51.8 181.9 %all-to-all-done = bf16[2,77,77,512]{3,2,1,0:T(8,128)(2,1)} async-done(((bf16[2,77,77,512]{3,2,1,0:T(8,128)(2,1)}), bf16[2,77,77,512]{3,2,1,0:T(8,128)(2,1)}, u32[]{:S(2)}, u32[]{:S(2)}) %all-to-all-start) | async-done | bytes 12142624 | tf_op jit(solution)/shard_map/all_to_all | solution.py:10
  233.7 18.1 %copy.13 = bf16[77,77,2,512]{3,2,1,0:T(2,128)(2,1)S(1)} copy(bf16[77,77,2,512]{3,1,0,2:T(8,128)(2,1)} %bitcast.1) | data formatting | bytes 24285184 | tf_op jit(solution)/shard_map/reshape | solution.py:9
  251.8 11.3 %pad.2 = bf16[5936,2,512]{2,1,0:T(2,128)(2,1)S(1)} pad(bf16[5929,2,512]{2,1,0:T(2,128)(2,1)S(1)} %bitcast.20, bf16[]{:T(256)} %constant.31), padding=0_7x0_0x0_0 | pad | bytes 24299522
  263.1 2.5 copy.18
  265.7 8.0 %fusion.8 = f32[1024,512]{1,0:T(8,128)} fusion(bf16[5929,1024]{1,0:T(8,128)(2,1)S(1)} %bitcast.21, bf16[5929,512]{1,0:T(8,128)(2,1)S(1)} %bitcast.25), kind=kOutput, calls=%fused_computation.10 | convolution fusion | flops 6217007104 | bytes 20311040 | tf_op jit(solution)/shard_map/dot_general | solution.py:37
  273.7 0.0 reduce-scatter.3.cloned.1.call-update
  273.7 0.2 reduce-scatter.5.cloned.1.call-start
  273.9 0.0 all-gather.2.cloned.1.call-done
  274.0 34.7 %fusion.3 = f32[77,16,2048]{2,1,0:T(8,128)} fusion(bf16[77,32,2048]{2,0,1:T(8,128)(2,1)} %all-gather.2.cloned.1.call-done, bf16[77,16,77,32]{2,3,1,0:T(8,128)(2,1)} %bitcast.22), kind=kOutput, calls=%fused_computation.4 | convolution fusion | flops 12434014208 | bytes 26256384 | tf_op jit(solution)/shard_map/dot_general | solution.py:55
  308.7 0.0 copy-start
  308.7 0.0 reduce-scatter.5.cloned.1.call-update
  308.7 0.6 copy-done.3
  309.3 0.1 dynamic_slice.9
  309.4 0.1 broadcast_add_fusion
  309.4 0.1 add.57
  309.5 0.1 dynamic_slice.11
  309.6 0.1 broadcast_subtract_fusion.1
  309.7 0.1 sub.60
  309.8 0.8 dynamic_slice.10
  310.5 0.1 broadcast_subtract_fusion
  310.6 289.1 %reduce-scatter.3.cloned.1.call-done = f32[16,512]{1,0:T(8,128)} async-done(((f32[1024,512]{1,0:T(8,128)}), f32[16,512]{1,0:T(8,128)}) %reduce-scatter.3.cloned.1.call-update) | async-done | bytes 32784 | tf_op jit(solution)/shard_map/reduce_scatter | solution.py:43
  599.7 1.5 subtract_divide_fusion
  601.1 65.8 %reduce-scatter.5.cloned.1.call-done = f32[77,16,256]{2,1,0:T(8,128)} async-done(((f32[77,16,2048]{2,1,0:T(8,128)}), f32[77,16,256]{2,1,0:T(8,128)}) %reduce-scatter.5.cloned.1.call-update) | async-done | bytes 1261584 | tf_op jit(solution)/shard_map/reduce_scatter | solution.py:61
  666.9 2.6 add_divide_fusion
  (13 shorter events, 0.0 us)
Async XLA Ops:
  8.0 266.0 %all-gather.2.cloned.1.call-start = ((), (), s32[]{:S(2)}) async-start(), calls=%async_computation.4 | async-start | bytes 11796480 | tf_op jit(solution)/shard_map/all_gather | solution.py:54
  22.3 211.4 %all-to-all-start = ((bf16[2,77,77,512]{3,2,1,0:T(8,128)(2,1)}), bf16[2,77,77,512]{3,2,1,0:T(8,128)(2,1)}, u32[]{:S(2)}, u32[]{:S(2)}) async-start(bf16[2,77,77,512]{3,2,1,0:T(8,128)(2,1)} %pad_maximum_fusion), calls=%async_computation | async-start | bytes 25231360 | tf_op jit(solution)/shard_map/all_to_all | solution.py:10
  31.3 568.3 %reduce-scatter.3.cloned.1.call-start = ((), (), s32[]{:S(2)}) async-start(), calls=%async_computation.3 | async-start | bytes 2129920 | tf_op jit(solution)/shard_map/reduce_scatter | solution.py:43
  251.8 13.9 %slice-start = ((s8[6078464]{0:T(1024)(128)(4,1)}), s8[4194304]{0:T(1024)(128)(4,1)S(1)}, s32[]{:S(2)}) async-start(s8[6078464]{0:T(1024)(128)(4,1)} %bitcast.24), calls=%async_computation.6 | async-start | bytes 8388608
  263.1 2.6 slice-start.1
  273.7 393.2 %reduce-scatter.5.cloned.1.call-start = ((), (), s32[]{:S(2)}) async-start(), calls=%async_computation.5 | async-start | bytes 11354112 | tf_op jit(solution)/shard_map/reduce_scatter | solution.py:61
  308.6 0.7 copy-start.3
  308.6 1.0 copy-start.4
  308.6 291.0 %copy-start.1 = (f32[16,512]{1,0:T(8,128)S(1)}, f32[16,512]{1,0:T(8,128)}, u32[]{:S(2)}) copy-start(f32[16,512]{1,0:T(8,128)} %param.12) | copy-start | bytes 98308
  308.7 291.0 %copy-start.2 = (f32[16]{0:T(128)S(1)}, f32[16]{0:T(128)}, u32[]{:S(2)}) copy-start(f32[16]{0:T(128)} %param.16) | copy-start | bytes 196
  308.7 358.2 %copy-start = (f32[77,16,256]{2,1,0:T(8,128)S(1)}, f32[77,16,256]{2,1,0:T(8,128)}, u32[]{:S(2)}) copy-start(f32[77,16,256]{2,1,0:T(8,128)} %param.13) | copy-start | bytes 3784708
Sparse Core Ops, SparseCore 0:
  11.2 205.5 all-gather.1
Sparse Core Ops, SparseCore 1:
  273.8 325.8 reduce-scatter.2
  602.1 64.7 reduce-scatter.4
